TPU v7x, 256 devices: a whole 4x4x8 slice. The times are simulated.
256 devices in a mesh: tm: 64 (over y_hi, z, x), head: 4 (over y_lo, core).
Axes of the slice: x: 4, y: 4 (y_hi: 2, y_lo: 2; y = y_hi * 2 + y_lo), z: 8, core: 2. Of those that a mesh axis runs over, the one named last changes fastest.
Arguments:
- frames: bfloat16 [64, 512, 1152], P('tm', None, 'head'), may hold values from -6 to 6
- modulation: float32 [3, 1152], replicated, may hold values from -4 to 4
- w_qkv: bfloat16 [3, 1152, 1152], P(None, None, 'head'), may hold values from -1 to 1
- w_out: bfloat16 [1152, 1152], P('head'), may hold values from -0.375 to 0.375
- conv_taps: float32 [3, 1152], P(None, 'head'), may hold values from -3 to 3
- anchors: int32 [4], replicated, may hold values from 0 to 15
Outputs:
- block_out: bfloat16 [64, 512, 1152], P('tm', None, 'head')
All inputs are finite; a program needn't handle non-finite values.
Results may differ from a plain program's by a relative error of at most 0.011.
Values may be sent and summed in bfloat16 or wider, within the bound.
A program may use at most 64 MiB of HBM per device.

v0:
```python
import jax
import jax.numpy as jnp
from jax import lax
from jax.sharding import PartitionSpec as P

HS = 72
SEG = 16
EPSILON = 1e-06


def swapped(block, axis, stride):
    count = lax.axis_size(axis)
    route = []
    for low in range(count):
        high = low | 1 << stride
        if high != low and high < count:
            route += [(low, high), (high, low)]
    return lax.ppermute(block, axis, route)


def extended(x, sides, width):
    for axis, dim in sides:
        size, length = (lax.axis_size(axis), x.shape[dim])
        up = [(i, (i + 1) % size) for i in range(size - 1)]
        down = [(j, i) for i, j in up]
        last = lax.slice_in_dim(x, length - width, length, axis=dim)
        leading = lax.slice_in_dim(x, 0, width, axis=dim)
        before = lax.ppermute(last, axis, up)
        after = lax.ppermute(leading, axis, down)
        x = jnp.concatenate([before, x, after], axis=dim)
    return x


def modulate(frame_rows, modulation):
    values = frame_rows.astype(jnp.float32)
    average = jnp.mean(values, axis=-1, keepdims=True)
    centred = values - average
    variance = jnp.mean(centred * centred, axis=-1, keepdims=True)
    normed = centred * lax.rsqrt(variance + EPSILON)
    return (normed * (1.0 + modulation[1]) + modulation[0]).astype(jnp.bfloat16)


def attend_block(queries, key_rows, value_rows):
    scores = jnp.einsum(
        "qhs,khs->hqk", queries, key_rows, preferred_element_type=jnp.float32
    ) * HS ** (-0.5)
    row_max = jnp.max(scores, axis=-1, keepdims=True)
    weights = jnp.exp(scores - row_max)
    weights = (weights / jnp.sum(weights, axis=-1, keepdims=True)).astype(jnp.bfloat16)
    return jnp.einsum(
        "hqk,khs->qhs", weights, value_rows, preferred_element_type=jnp.float32
    ).astype(jnp.bfloat16)


def local(frames, modulation, w_qkv, w_out, conv_taps, anchors):
    local_frames, tokens, width_dev = frames.shape
    group_size = SEG // local_frames
    tm_pos = lax.axis_index("tm")
    head_pos = lax.axis_index("head")
    gathered = lax.all_gather(frames, "head", axis=2, tiled=True)
    normed = modulate(gathered, modulation)
    projections = jnp.einsum(
        "fpd,cde->cfpe", normed, w_qkv, preferred_element_type=jnp.float32
    ).astype(jnp.bfloat16)
    segment = tm_pos * local_frames // SEG
    anchor_frame = segment * SEG + lax.dynamic_index_in_dim(anchors, segment, 0, keepdims=False)
    is_owner = anchor_frame // local_frames == tm_pos
    anchor_local = anchor_frame % local_frames
    own_part = lax.dynamic_index_in_dim(projections[1:], anchor_local, 1, keepdims=False)
    routed = jnp.where(is_owner, own_part, jnp.zeros_like(own_part))
    for bit_pos in range(group_size.bit_length() - 1):
        routed = routed + swapped(routed, "tm", bit_pos)
    heads_dev = width_dev // HS
    block_rows = min(512, tokens)
    anchor_keys = routed[0].reshape(tokens, heads_dev, HS)
    anchor_values = routed[1].reshape(tokens, heads_dev, HS)

    def frame_attention(pieces):
        queries, own_keys, own_values = pieces
        key_rows = jnp.concatenate([own_keys.reshape(tokens, heads_dev, HS), anchor_keys], axis=0)
        value_rows = jnp.concatenate(
            [own_values.reshape(tokens, heads_dev, HS), anchor_values], axis=0
        )
        query_blocks = queries.reshape(tokens // block_rows, block_rows, heads_dev, HS)

        def one_block(block_queries):
            return attend_block(block_queries, key_rows, value_rows)

        outputs = lax.map(one_block, query_blocks)
        return outputs.reshape(tokens, width_dev)

    attended = lax.map(frame_attention, (projections[0], projections[1], projections[2]))
    partial_terms = jnp.einsum("fpe,ed->fpd", attended, w_out, preferred_element_type=jnp.float32)
    summed = lax.psum_scatter(partial_terms, "head", scatter_dimension=2, tiled=True)
    gate_dev = lax.dynamic_slice_in_dim(modulation[2], head_pos * width_dev, width_dev)
    hidden = (frames.astype(jnp.float32) + gate_dev * summed).astype(jnp.bfloat16)
    padded = extended(hidden, (("tm", 0),), 1).astype(jnp.float32)
    block_out = (
        padded[1:-1]
        + conv_taps[0] * padded[:-2]
        + conv_taps[1] * padded[1:-1]
        + conv_taps[2] * padded[2:]
    )
    return block_out.astype(jnp.bfloat16)


def solution(mesh):
    in_specs = (
        P("tm", None, "head"),
        P(),
        P(None, None, "head"),
        P("head", None),
        P(None, "head"),
        P(),
    )
    out_specs = P("tm", None, "head")
    return jax.shard_map(local, mesh=mesh, in_specs=in_specs, out_specs=out_specs, check_vma=False)
```

profile of v0, /device:TPU:230, one launch (start us, length us, event | category | flops | bytes accessed | tf_op | source)
XLA Modules:
  0.0 228.0 jit_solution(18161637918810966751)
XLA Ops:
  7.3 1.2 dynamic_slice.21
  10.1 23.4 %all-gather.2.cloned.1.call-done = bf16[1,512,1152]{1,2,0:T(8,128)(2,1)} async-done(((bf16[1,512,288]{1,2,0:T(8,128)(2,1)}), bf16[1,512,1152]{1,2,0:T(8,128)(2,1)}) %all-gather.2.cloned.1.call-update) | async-done | bytes 1179664 | tf_op jit(solution)/shard_map/all_gather | solution.py:60
  33.5 1.6 convert_reduce_fusion
  35.1 1.6 fusion.8
  36.7 1.4 fusion.12
  38.2 0.9 collective-permute-start
  39.1 14.8 %collective-permute-done = bf16[2,512,288]{1,2,0:T(8,128)(2,1)S(1)} collective-permute-done((bf16[2,512,288]{1,2,0:T(8,128)(2,1)S(1)}, bf16[2,512,288]{1,2,0:T(8,128)(2,1)S(1)}, u32[]{:S(2)}, u32[]{:S(2)}) %collective-permute-start) | collective-permute-done | bytes 589856 | tf_op jit(solution)/shard_map/ppermute | solution.py:18
  54.0 1.5 collective-permute-start.1
  55.6 14.9 %collective-permute-done.1 = bf16[2,512,288]{1,2,0:T(8,128)(2,1)S(1)} collective-permute-done((bf16[2,512,288]{1,2,0:T(8,128)(2,1)S(1)}, bf16[2,512,288]{1,2,0:T(8,128)(2,1)S(1)}, u32[]{:S(2)}, u32[]{:S(2)}) %collective-permute-start.1) | collective-permute-done | bytes 589856 | tf_op jit(solution)/shard_map/ppermute | solution.py:18
  70.6 1.4 collective-permute-start.2
  72.0 12.6 %collective-permute-done.2 = bf16[2,512,288]{1,2,0:T(8,128)(2,1)S(1)} collective-permute-done((bf16[2,512,288]{1,2,0:T(8,128)(2,1)S(1)}, bf16[2,512,288]{1,2,0:T(8,128)(2,1)S(1)}, u32[]{:S(2)}, u32[]{:S(2)}) %collective-permute-start.2) | collective-permute-done | bytes 589856 | tf_op jit(solution)/shard_map/ppermute | solution.py:18
  84.8 2.3 collective-permute-start.3
  87.1 24.4 %collective-permute-done.3 = bf16[2,512,288]{1,2,0:T(8,128)(2,1)S(1)} collective-permute-done((bf16[2,512,288]{1,2,0:T(8,128)(2,1)S(1)}, bf16[2,512,288]{1,2,0:T(8,128)(2,1)S(1)}, u32[]{:S(2)}, u32[]{:S(2)}) %collective-permute-start.3) | collective-permute-done | bytes 589856 | tf_op jit(solution)/shard_map/ppermute | solution.py:18
  111.7 5.0 %fusion.41 = (f32[4,512]{1,0:T(4,128)S(1)}, f32[4,512,1024]{2,1,0:T(8,128)}) fusion(bf16[512,4,72]{0,2,1:T(8,128)(2,1)S(1)} %bitcast.35, bf16[512,4,72]{0,2,1:T(8,128)(2,1)S(1)} %bitcast.37, bf16[512,4,72]{0,2,1:T(8,128)(2,1)S(1)} %bitcast.34), kind=kOutput, calls=%fused_computation.57 | convolution fusion | flops 309462016 | bytes 9281536 | tf_op jit(solution)/shard_map/while/body/eval_jaxpr/while/body/eval_jaxpr/sub | solution.py:48
  116.7 4.9 %fusion.13 = bf16[4,72,512]{2,1,0:T(8,128)(2,1)S(1)} fusion(f32[4,512,1024]{2,1,0:T(8,128)} %get-tuple-element.58, f32[4,512]{1,0:T(4,128)S(1)} %get-tuple-element.57, bf16[512,4,72]{0,2,1:T(8,128)(2,1)S(1)} %bitcast.36, bf16[512,4,72]{0,2,1:T(8,128)(2,1)S(1)} %bitcast.33), kind=kOutput, calls=%fused_computation.18 | convolution fusion | flops 307511296 | bytes 9281536 | tf_op jit(solution)/shard_map/while/body/eval_jaxpr/while/body/eval_jaxpr/hqk,khs->qhs/dot_general | solution.py:50
  121.6 2.2 convolution_bitcast_fusion
  123.8 6.4 %copy.23 = f32[1,512,1152]{1,0,2:T(1,128)} copy(f32[1,512,1152]{2,1,0:T(8,128)} %convolution_bitcast_fusion) | data formatting | bytes 4718592 | tf_op jit(solution)/shard_map/fpe,ed->fpd/dot_general | solution.py:93
  132.2 65.7 %all-reduce.3.cloned.1.call-done = f32[1,512,1152]{1,0,2:T(1,128)} async-done(((f32[1,512,1152]{1,0,2:T(1,128)}), f32[1,512,1152]{1,0,2:T(1,128)}) %all-reduce.3.cloned.1.call-update) | async-done | bytes 2359312
  197.9 1.5 constant_dynamic-slice_fusion
  199.5 4.0 %collective-permute-start.4 = (bf16[1,512,288]{1,2,0:T(8,128)(2,1)S(1)}, bf16[1,512,288]{1,2,0:T(8,128)(2,1)S(1)}, u32[]{:S(2)}, u32[]{:S(2)}) collective-permute-start(bf16[1,512,288]{1,2,0:T(8,128)(2,1)S(1)} %fusion.31), channel_id=1, source_target_pairs={{0,4},{4,8},{8,12},{12,16},{16,20},{20,24},{24,28},{28,32},{32,36}... | collective-permute-start | bytes 884744 | tf_op jit(solution)/shard_map/ppermute | solution.py:28
  203.5 1.9 collective-permute-start.5
  205.5 5.2 %collective-permute-done.4 = bf16[1,512,288]{1,2,0:T(8,128)(2,1)S(1)} collective-permute-done((bf16[1,512,288]{1,2,0:T(8,128)(2,1)S(1)}, bf16[1,512,288]{1,2,0:T(8,128)(2,1)S(1)}, u32[]{:S(2)}, u32[]{:S(2)}) %collective-permute-start.4) | collective-permute-done | bytes 294944 | tf_op jit(solution)/shard_map/ppermute | solution.py:28
  210.7 9.4 %collective-permute-done.5 = bf16[1,512,288]{1,2,0:T(8,128)(2,1)S(1)} collective-permute-done((bf16[1,512,288]{1,2,0:T(8,128)(2,1)S(1)}, bf16[1,512,288]{1,2,0:T(8,128)(2,1)S(1)}, u32[]{:S(2)}, u32[]{:S(2)}) %collective-permute-start.5) | collective-permute-done | bytes 294944 | tf_op jit(solution)/shard_map/ppermute | solution.py:29
  220.2 0.9 fusion.23
  (31 shorter events, 4.0 us)
Async XLA Ops:
  6.5 30.2 %copy-start = (bf16[3,1152,288]{1,2,0:T(8,128)(2,1)S(1)}, bf16[3,1152,288]{1,2,0:T(8,128)(2,1)}, u32[]{:S(2)}) copy-start(bf16[3,1152,288]{1,2,0:T(8,128)(2,1)} %param.8) | copy-start | bytes 5971972
  6.5 26.9 %all-gather.2.cloned.1.call-start = ((), (), s32[]{:S(2)}) async-start(), calls=%async_computation | async-start | bytes 1474560 | tf_op jit(solution)/shard_map/all_gather | solution.py:60
  7.3 190.6 %all-reduce.3.cloned.1.call-start = ((), (), s32[]{:S(2)}) async-start(), calls=%async_computation.1 | async-start | bytes 4718592
  33.5 3.3 %copy-start.1 = (bf16[1,512,1152]{1,2,0:T(8,128)(2,1)S(1)}, bf16[1,512,1152]{1,2,0:T(8,128)(2,1)}, u32[]{:S(2)}) copy-start(bf16[1,512,1152]{1,2,0:T(8,128)(2,1)} %all-gather.2.cloned.1.call-done) | copy-start | bytes 3538948
  38.2 15.7 %collective-permute-start = (bf16[2,512,288]{1,2,0:T(8,128)(2,1)S(1)}, bf16[2,512,288]{1,2,0:T(8,128)(2,1)S(1)}, u32[]{:S(2)}, u32[]{:S(2)}) collective-permute-start(bf16[2,512,288]{1,2,0:T(8,128)(2,1)S(1)} %fusion.26), channel_id=1, source_target_pairs={{0,4},{4,0},{8,12},{12,8},{16,20},{20,16},{24,28},{28,24},{32,36},... | collective-permute-start | bytes 1769480 | tf_op jit(solution)/shard_map/ppermute | solution.py:18
  54.0 16.4 %collective-permute-start.1 = (bf16[2,512,288]{1,2,0:T(8,128)(2,1)S(1)}, bf16[2,512,288]{1,2,0:T(8,128)(2,1)S(1)}, u32[]{:S(2)}, u32[]{:S(2)}) collective-permute-start(bf16[2,512,288]{1,2,0:T(8,128)(2,1)S(1)} %fusion.47), channel_id=1, source_target_pairs={{0,8},{8,0},{4,12},{12,4},{16,24},{24,16},{20,28},{28,20},{32,40},... | collective-permute-start | bytes 1769480 | tf_op jit(solution)/shard_map/ppermute | solution.py:18
  70.6 14.0 %collective-permute-start.2 = (bf16[2,512,288]{1,2,0:T(8,128)(2,1)S(1)}, bf16[2,512,288]{1,2,0:T(8,128)(2,1)S(1)}, u32[]{:S(2)}, u32[]{:S(2)}) collective-permute-start(bf16[2,512,288]{1,2,0:T(8,128)(2,1)S(1)} %add.93), channel_id=1, source_target_pairs={{0,16},{16,0},{4,20},{20,4},{8,24},{24,8},{12,28},{28,12},{32,48},... | collective-permute-start | bytes 1769480 | tf_op jit(solution)/shard_map/ppermute | solution.py:18
  84.8 26.7 %collective-permute-start.3 = (bf16[2,512,288]{1,2,0:T(8,128)(2,1)S(1)}, bf16[2,512,288]{1,2,0:T(8,128)(2,1)S(1)}, u32[]{:S(2)}, u32[]{:S(2)}) collective-permute-start(bf16[2,512,288]{1,2,0:T(8,128)(2,1)S(1)} %add.94), channel_id=1, source_target_pairs={{0,32},{32,0},{4,36},{36,4},{8,40},{40,8},{12,44},{44,12},{16,48},... | collective-permute-start | bytes 1769480 | tf_op jit(solution)/shard_map/ppermute | solution.py:18
  116.7 4.9 %copy-start.3 = (bf16[288,1152]{1,0:T(8,128)(2,1)S(1)}, bf16[288,1152]{1,0:T(8,128)(2,1)}, u32[]{:S(2)}) copy-start(bf16[288,1152]{1,0:T(8,128)(2,1)} %param.9) | copy-start | bytes 1990660
  130.2 0.7 copy-start.5
  130.2 69.2 %copy-start.2 = (bf16[1,512,288]{1,2,0:T(8,128)(2,1)S(1)}, bf16[1,512,288]{1,2,0:T(8,128)(2,1)}, u32[]{:S(2)}) copy-start(bf16[1,512,288]{1,2,0:T(8,128)(2,1)} %param.6) | copy-start | bytes 884740
  130.2 75.2 %copy-start.4 = (f32[3,288]{1,0:T(4,128)S(1)}, f32[3,288]{1,0:T(4,128)}, u32[]{:S(2)}) copy-start(f32[3,288]{1,0:T(4,128)} %param.10) | copy-start | bytes 10372
  199.5 11.2 %collective-permute-start.4 = (bf16[1,512,288]{1,2,0:T(8,128)(2,1)S(1)}, bf16[1,512,288]{1,2,0:T(8,128)(2,1)S(1)}, u32[]{:S(2)}, u32[]{:S(2)}) collective-permute-start(bf16[1,512,288]{1,2,0:T(8,128)(2,1)S(1)} %fusion.31), channel_id=1, source_target_pairs={{0,4},{4,8},{8,12},{12,16},{16,20},{20,24},{24,28},{28,32},{32,36}... | collective-permute-start | bytes 884744 | tf_op jit(solution)/shard_map/ppermute | solution.py:28
  203.5 16.6 %collective-permute-start.5 = (bf16[1,512,288]{1,2,0:T(8,128)(2,1)S(1)}, bf16[1,512,288]{1,2,0:T(8,128)(2,1)S(1)}, u32[]{:S(2)}, u32[]{:S(2)}) collective-permute-start(bf16[1,512,288]{1,2,0:T(8,128)(2,1)S(1)} %fusion.31), channel_id=1, source_target_pairs={{4,0},{8,4},{12,8},{16,12},{20,16},{24,20},{28,24},{32,28},{36,32}... | collective-permute-start | bytes 884744 | tf_op jit(solution)/shard_map/ppermute | solution.py:29
Sparse Core Ops, SparseCore 0:
  9.1 24.2 all-gather.1
  130.4 67.4 all-reduce.2
where the time goes:
time: 228 us
  waiting for transfers between devices  171 us (75%)
  between operations  14.9 us (7%)
  matrix products  13.5 us (6%)
  starting transfers between devices  12.1 us (5%)
  local copies, waits for them, and re-layouts  10.6 us (5%)
  other arithmetic  5.89 us (3%)
    ppermute x4, waiting for transfers between devices, swapped(): return lax.ppermute(block, axis, route)  66.7 us
    unnamed x3, waiting for transfers between devices  66.4 us
    all_gather x1, waiting for transfers between devices, local(): gathered = lax.all_gather(frames, 'head', axis=2, tiled=True)  23.4 us
    ppermute x1, waiting for transfers between devices, extended(): after = lax.ppermute(leading, axis, down)  9.42 us
    dot_general x1, local copies, waits for them, and re-layouts, local(): jnp.einsum('fpe,ed->fpd', attended, w_out, preferred_element_type=jnp.flo...  6.39 us
    ppermute x4, starting transfers between devices, swapped(): return lax.ppermute(block, axis, route)  6.18 us
    ppermute x1, waiting for transfers between devices, extended(): before = lax.ppermute(last, axis, up)  5.21 us
    sub x1, matrix products, attend_block(): weights = jnp.exp(scores - row_max)  4.96 us
  transfers between devices with their start and end apart: 8, of which 8 were waited for; matrix products, arithmetic and copies ran while one was open for 1% of the time, Pallas kernels for 0%

commit v1 on v0

--- a/solution.py
+++ b/solution.py
@@ -2,10 +2,23 @@
 import jax.numpy as jnp
 from jax import lax
 from jax.sharding import PartitionSpec as P
+from jax.lax import all_to_all, psum
 
 HS = 72
 SEG = 16
 EPSILON = 1e-06
+
+
+def _extend_rows(inp, chip_axis):
+    return jnp.concatenate(
+        all_to_all(
+            jnp.stack(tuple((inp for _ in range(psum(1, axis_name=chip_axis)))), axis=0),
+            axis_name=chip_axis,
+            split_axis=0,
+            concat_axis=0,
+        ),
+        axis=2,
+    )
 
 
 def swapped(block, axis, stride):
@@ -57,7 +70,7 @@
     group_size = SEG // local_frames
     tm_pos = lax.axis_index("tm")
     head_pos = lax.axis_index("head")
-    gathered = lax.all_gather(frames, "head", axis=2, tiled=True)
+    gathered = _extend_rows(frames, "head")
     normed = modulate(gathered, modulation)
     projections = jnp.einsum(
         "fpd,cde->cfpe", normed, w_qkv, preferred_element_type=jnp.float32

time: 228 us -> 217 us (0.952)
  waiting for transfers between devices: 171 us -> 159 us
  other arithmetic: 5.89 us -> 3.09 us
  starting transfers between devices: 12.1 us -> 14.5 us
    all_gather x1 -> x0, waiting for transfers between devices: 23.4 us -> none  [local(): gathered = lax.all_gather(frames, 'head', axis=2, tiled=True)]
    all_to_all x0 -> x1, waiting for transfers between devices: none -> 14.4 us  [_extend_rows(): all_to_all(jnp.stack(tuple((inp for _ in range(psum(1, axis_name=chip_axi...]
    all_to_all x0 -> x1, starting transfers between devices: none -> 3.53 us  [_extend_rows(): all_to_all(jnp.stack(tuple((inp for _ in range(psum(1, axis_name=chip_axi...]
    ppermute x4, waiting for transfers between devices: 66.7 us -> 64.2 us  [swapped(): return lax.ppermute(block, axis, route)]
    unnamed x3 -> x2, waiting for transfers between devices: 66.4 us -> 65.5 us
where the time goes in v1:
time: 217 us
  waiting for transfers between devices  159 us (73%)
  between operations  14.9 us (7%)
  starting transfers between devices  14.5 us (7%)
  matrix products  13.4 us (6%)
  local copies, waits for them, and re-layouts  12.1 us (6%)
  other arithmetic  3.09 us (1%)
    unnamed x2, waiting for transfers between devices  65.5 us
    ppermute x4, waiting for transfers between devices, swapped(): return lax.ppermute(block, axis, route)  64.2 us
    all_to_all x1, waiting for transfers between devices, _extend_rows(): all_to_all(jnp.stack(tuple((inp for _ in range(psum(1, axis_name=chip_axi...  14.4 us
    ppermute x1, waiting for transfers between devices, extended(): after = lax.ppermute(leading, axis, down)  9.42 us
    dot_general x1, local copies, waits for them, and re-layouts, local(): jnp.einsum('fpe,ed->fpd', attended, w_out, preferred_element_type=jnp.flo...  6.39 us
    ppermute x1, waiting for transfers between devices, extended(): before = lax.ppermute(last, axis, up)  5.21 us
    ppermute x4, starting transfers between devices, swapped(): return lax.ppermute(block, axis, route)  5.04 us
    sub x1, matrix products, attend_block(): weights = jnp.exp(scores - row_max)  4.96 us
  transfers between devices with their start and end apart: 8, of which 8 were waited for; matrix products, arithmetic and copies ran while one was open for 1% of the time, Pallas kernels for 0%

profile of v1, /device:TPU:230, one launch (start us, length us, event | category | flops | bytes accessed | tf_op | source)
XLA Modules:
  0.0 216.8 jit_solution(958786207511863751)
XLA Ops:
  6.5 2.2 %stack.2 = bf16[4,1,512,288]{2,3,1,0:T(8,128)(2,1)} broadcast(bf16[512,288]{0,1:T(8,128)(2,1)} %bitcast.54), dimensions={2,3} | broadcast | bytes 1474560 | tf_op jit(solution)/shard_map/stack | solution.py:15
  8.7 3.5 %all-to-all-start = ((bf16[4,1,512,288]{2,3,1,0:T(8,128)(2,1)}), bf16[4,1,512,288]{2,3,1,0:T(8,128)(2,1)S(1)}, u32[]{:S(2)}, u32[]{:S(2)}) async-start(bf16[4,1,512,288]{2,3,1,0:T(8,128)(2,1)} %stack.2), calls=%async_computation | async-start | bytes 2359296 | tf_op jit(solution)/shard_map/all_to_all | solution.py:14
  13.7 14.4 %all-to-all-done = bf16[4,1,512,288]{2,3,1,0:T(8,128)(2,1)S(1)} async-done(((bf16[4,1,512,288]{2,3,1,0:T(8,128)(2,1)}), bf16[4,1,512,288]{2,3,1,0:T(8,128)(2,1)S(1)}, u32[]{:S(2)}, u32[]{:S(2)}) %all-to-all-start) | async-done | bytes 1179680 | tf_op jit(solution)/shard_map/all_to_all | solution.py:14
  29.4 1.3 fusion.12
  30.8 0.9 collective-permute-start
  31.7 13.9 %collective-permute-done = bf16[2,512,288]{1,2,0:T(8,128)(2,1)S(1)} collective-permute-done((bf16[2,512,288]{1,2,0:T(8,128)(2,1)S(1)}, bf16[2,512,288]{1,2,0:T(8,128)(2,1)S(1)}, u32[]{:S(2)}, u32[]{:S(2)}) %collective-permute-start) | collective-permute-done | bytes 589856 | tf_op jit(solution)/shard_map/ppermute | solution.py:31
  45.7 1.5 collective-permute-start.1
  47.2 14.0 %collective-permute-done.1 = bf16[2,512,288]{1,2,0:T(8,128)(2,1)S(1)} collective-permute-done((bf16[2,512,288]{1,2,0:T(8,128)(2,1)S(1)}, bf16[2,512,288]{1,2,0:T(8,128)(2,1)S(1)}, u32[]{:S(2)}, u32[]{:S(2)}) %collective-permute-start.1) | collective-permute-done | bytes 589856 | tf_op jit(solution)/shard_map/ppermute | solution.py:31
  61.4 1.1 collective-permute-start.2
  62.5 12.1 %collective-permute-done.2 = bf16[2,512,288]{1,2,0:T(8,128)(2,1)S(1)} collective-permute-done((bf16[2,512,288]{1,2,0:T(8,128)(2,1)S(1)}, bf16[2,512,288]{1,2,0:T(8,128)(2,1)S(1)}, u32[]{:S(2)}, u32[]{:S(2)}) %collective-permute-start.2) | collective-permute-done | bytes 589856 | tf_op jit(solution)/shard_map/ppermute | solution.py:31
  74.7 1.5 collective-permute-start.3
  76.3 24.2 %collective-permute-done.3 = bf16[2,512,288]{1,2,0:T(8,128)(2,1)S(1)} collective-permute-done((bf16[2,512,288]{1,2,0:T(8,128)(2,1)S(1)}, bf16[2,512,288]{1,2,0:T(8,128)(2,1)S(1)}, u32[]{:S(2)}, u32[]{:S(2)}) %collective-permute-start.3) | collective-permute-done | bytes 589856 | tf_op jit(solution)/shard_map/ppermute | solution.py:31
  100.7 5.0 %fusion.37 = (f32[4,512]{1,0:T(4,128)S(1)}, f32[4,512,1024]{2,1,0:T(8,128)}) fusion(bf16[512,4,72]{0,2,1:T(8,128)(2,1)S(1)} %bitcast.58, bf16[512,4,72]{0,2,1:T(8,128)(2,1)S(1)} %bitcast.60, bf16[512,4,72]{0,2,1:T(8,128)(2,1)S(1)} %bitcast.57), kind=kOutput, calls=%fused_computation.55 | convolution fusion | flops 309462016 | bytes 9281536 | tf_op jit(solution)/shard_map/while/body/eval_jaxpr/while/body/eval_jaxpr/sub | solution.py:61
  105.7 4.9 %fusion.13 = bf16[4,72,512]{2,1,0:T(8,128)(2,1)S(1)} fusion(f32[4,512,1024]{2,1,0:T(8,128)} %get-tuple-element.58, f32[4,512]{1,0:T(4,128)S(1)} %get-tuple-element.57, bf16[512,4,72]{0,2,1:T(8,128)(2,1)S(1)} %bitcast.59, bf16[512,4,72]{0,2,1:T(8,128)(2,1)S(1)} %bitcast.56), kind=kOutput, calls=%fused_computation.18 | convolution fusion | flops 307511296 | bytes 9281536 | tf_op jit(solution)/shard_map/while/body/eval_jaxpr/while/body/eval_jaxpr/hqk,khs->qhs/dot_general | solution.py:63
  110.6 2.3 %convolution_bitcast_fusion = f32[1,512,1152]{2,1,0:T(8,128)} fusion(bf16[512,288]{0,1:T(8,128)(2,1)S(1)} %bitcast.55, bf16[288,1152]{1,0:T(8,128)(2,1)S(1)} %copy-done.2), kind=kOutput, calls=%fused_computation.7 | convolution fusion | flops 339738624 | bytes 3317760 | tf_op jit(solution)/shard_map/fpe,ed->fpd/dot_general | solution.py:106
  112.8 6.4 %copy.29 = f32[1,512,1152]{1,0,2:T(1,128)} copy(f32[1,512,1152]{2,1,0:T(8,128)} %convolution_bitcast_fusion) | data formatting | bytes 4718592 | tf_op jit(solution)/shard_map/fpe,ed->fpd/dot_general | solution.py:106
  119.3 0.6 copy-done.6
  121.2 65.4 %all-reduce.3.cloned.1.call-done = f32[1,512,1152]{1,0,2:T(1,128)} async-done(((f32[1,512,1152]{1,0,2:T(1,128)}), f32[1,512,1152]{1,0,2:T(1,128)}) %all-reduce.3.cloned.1.call-update) | async-done | bytes 2359312
  186.7 1.5 constant_dynamic-slice_fusion
  188.3 4.0 %collective-permute-start.4 = (bf16[1,512,288]{1,2,0:T(8,128)(2,1)S(1)}, bf16[1,512,288]{1,2,0:T(8,128)(2,1)S(1)}, u32[]{:S(2)}, u32[]{:S(2)}) collective-permute-start(bf16[1,512,288]{1,2,0:T(8,128)(2,1)S(1)} %fusion.27), channel_id=1, source_target_pairs={{0,4},{4,8},{8,12},{12,16},{16,20},{20,24},{24,28},{28,32},{32,36}... | collective-permute-start | bytes 884744 | tf_op jit(solution)/shard_map/ppermute | solution.py:41
  192.3 1.9 collective-permute-start.5
  194.3 5.2 %collective-permute-done.4 = bf16[1,512,288]{1,2,0:T(8,128)(2,1)S(1)} collective-permute-done((bf16[1,512,288]{1,2,0:T(8,128)(2,1)S(1)}, bf16[1,512,288]{1,2,0:T(8,128)(2,1)S(1)}, u32[]{:S(2)}, u32[]{:S(2)}) %collective-permute-start.4) | collective-permute-done | bytes 294944 | tf_op jit(solution)/shard_map/ppermute | solution.py:41
  199.5 9.4 %collective-permute-done.5 = bf16[1,512,288]{1,2,0:T(8,128)(2,1)S(1)} collective-permute-done((bf16[1,512,288]{1,2,0:T(8,128)(2,1)S(1)}, bf16[1,512,288]{1,2,0:T(8,128)(2,1)S(1)}, u32[]{:S(2)}, u32[]{:S(2)}) %collective-permute-start.5) | collective-permute-done | bytes 294944 | tf_op jit(solution)/shard_map/ppermute | solution.py:42
  209.0 0.9 fusion.19
  (35 shorter events, 3.6 us)
Async XLA Ops:
  6.5 22.9 %copy-start = (bf16[3,1152,288]{1,2,0:T(8,128)(2,1)S(1)}, bf16[3,1152,288]{1,2,0:T(8,128)(2,1)}, u32[]{:S(2)}) copy-start(bf16[3,1152,288]{1,2,0:T(8,128)(2,1)} %param.8) | copy-start | bytes 5971972
  6.5 5.8 %copy-start.5 = (s32[4]{0:T(128)S(1)}, s32[4]{0:T(128)}, u32[]{:S(2)}) copy-start(s32[4]{0:T(128)} %param.11) | copy-start | bytes 52
  6.5 7.1 %copy-start.3 = (f32[3,1152]{1,0:T(4,128)S(1)}, f32[3,1152]{1,0:T(4,128)}, u32[]{:S(2)}) copy-start(f32[3,1152]{1,0:T(4,128)} %param.7) | copy-start | bytes 41476
  8.7 19.3 %all-to-all-start = ((bf16[4,1,512,288]{2,3,1,0:T(8,128)(2,1)}), bf16[4,1,512,288]{2,3,1,0:T(8,128)(2,1)S(1)}, u32[]{:S(2)}, u32[]{:S(2)}) async-start(bf16[4,1,512,288]{2,3,1,0:T(8,128)(2,1)} %stack.2), calls=%async_computation | async-start | bytes 2359296 | tf_op jit(solution)/shard_map/all_to_all | solution.py:14
  12.3 174.4 %all-reduce.3.cloned.1.call-start = ((), (), s32[]{:S(2)}) async-start(), calls=%async_computation.1 | async-start | bytes 4718592
  30.8 14.9 %collective-permute-start = (bf16[2,512,288]{1,2,0:T(8,128)(2,1)S(1)}, bf16[2,512,288]{1,2,0:T(8,128)(2,1)S(1)}, u32[]{:S(2)}, u32[]{:S(2)}) collective-permute-start(bf16[2,512,288]{1,2,0:T(8,128)(2,1)S(1)} %fusion.22), channel_id=1, source_target_pairs={{0,4},{4,0},{8,12},{12,8},{16,20},{20,16},{24,28},{28,24},{32,36},... | collective-permute-start | bytes 1769480 | tf_op jit(solution)/shard_map/ppermute | solution.py:31
  45.7 15.5 %collective-permute-start.1 = (bf16[2,512,288]{1,2,0:T(8,128)(2,1)S(1)}, bf16[2,512,288]{1,2,0:T(8,128)(2,1)S(1)}, u32[]{:S(2)}, u32[]{:S(2)}) collective-permute-start(bf16[2,512,288]{1,2,0:T(8,128)(2,1)S(1)} %fusion.43), channel_id=1, source_target_pairs={{0,8},{8,0},{4,12},{12,4},{16,24},{24,16},{20,28},{28,20},{32,40},... | collective-permute-start | bytes 1769480 | tf_op jit(solution)/shard_map/ppermute | solution.py:31
  61.4 13.1 %collective-permute-start.2 = (bf16[2,512,288]{1,2,0:T(8,128)(2,1)S(1)}, bf16[2,512,288]{1,2,0:T(8,128)(2,1)S(1)}, u32[]{:S(2)}, u32[]{:S(2)}) collective-permute-start(bf16[2,512,288]{1,2,0:T(8,128)(2,1)S(1)} %add.93), channel_id=1, source_target_pairs={{0,16},{16,0},{4,20},{20,4},{8,24},{24,8},{12,28},{28,12},{32,48},... | collective-permute-start | bytes 1769480 | tf_op jit(solution)/shard_map/ppermute | solution.py:31
  74.7 25.8 %collective-permute-start.3 = (bf16[2,512,288]{1,2,0:T(8,128)(2,1)S(1)}, bf16[2,512,288]{1,2,0:T(8,128)(2,1)S(1)}, u32[]{:S(2)}, u32[]{:S(2)}) collective-permute-start(bf16[2,512,288]{1,2,0:T(8,128)(2,1)S(1)} %add.94), channel_id=1, source_target_pairs={{0,32},{32,0},{4,36},{36,4},{8,40},{40,8},{12,44},{44,12},{16,48},... | collective-permute-start | bytes 1769480 | tf_op jit(solution)/shard_map/ppermute | solution.py:31
  105.7 4.9 %copy-start.2 = (bf16[288,1152]{1,0:T(8,128)(2,1)S(1)}, bf16[288,1152]{1,0:T(8,128)(2,1)}, u32[]{:S(2)}) copy-start(bf16[288,1152]{1,0:T(8,128)(2,1)} %param.9) | copy-start | bytes 1990660
  119.2 0.7 copy-start.6
  119.2 68.9 %copy-start.1 = (bf16[1,512,288]{1,2,0:T(8,128)(2,1)S(1)}, bf16[1,512,288]{1,2,0:T(8,128)(2,1)}, u32[]{:S(2)}) copy-start(bf16[1,512,288]{1,2,0:T(8,128)(2,1)} %param.6) | copy-start | bytes 884740
  119.2 75.0 %copy-start.4 = (f32[3,288]{1,0:T(4,128)S(1)}, f32[3,288]{1,0:T(4,128)}, u32[]{:S(2)}) copy-start(f32[3,288]{1,0:T(4,128)} %param.10) | copy-start | bytes 10372
  188.3 11.2 %collective-permute-start.4 = (bf16[1,512,288]{1,2,0:T(8,128)(2,1)S(1)}, bf16[1,512,288]{1,2,0:T(8,128)(2,1)S(1)}, u32[]{:S(2)}, u32[]{:S(2)}) collective-permute-start(bf16[1,512,288]{1,2,0:T(8,128)(2,1)S(1)} %fusion.27), channel_id=1, source_target_pairs={{0,4},{4,8},{8,12},{12,16},{16,20},{20,24},{24,28},{28,32},{32,36}... | collective-permute-start | bytes 884744 | tf_op jit(solution)/shard_map/ppermute | solution.py:41
  192.3 16.6 %collective-permute-start.5 = (bf16[1,512,288]{1,2,0:T(8,128)(2,1)S(1)}, bf16[1,512,288]{1,2,0:T(8,128)(2,1)S(1)}, u32[]{:S(2)}, u32[]{:S(2)}) collective-permute-start(bf16[1,512,288]{1,2,0:T(8,128)(2,1)S(1)} %fusion.27), channel_id=1, source_target_pairs={{4,0},{8,4},{12,8},{16,12},{20,16},{24,20},{28,24},{32,28},{36,32}... | collective-permute-start | bytes 884744 | tf_op jit(solution)/shard_map/ppermute | solution.py:42
Sparse Core Ops, SparseCore 0:
  119.4 67.2 all-reduce.2
